TPU v7x, 512 devices: a whole 4x8x8 slice. The times are simulated.
512 devices in a mesh: batch: 32 (over z, y_hi), weight: 16 (over x, y_lo, core).
Axes of the slice: x: 4, y: 8 (y_hi: 4, y_lo: 2; y = y_hi * 2 + y_lo), z: 8, core: 2. Of those that a mesh axis runs over, the one named last changes fastest.
Arguments:
- tokens: bfloat16 [16384, 8192], P(('batch', 'weight')), may hold values from -6 to 6
- segment_ids: int32 [16384], P('batch'), may hold values from 0 to 511, never falling along the last dimension, each value on 1 to 64 neighbouring positions
- norm_gain: float32 [8192], replicated, may hold values from 0.1 to 1.9
- query_weight: bfloat16 [8192, 8192], P('batch', 'weight'), may hold values from -0.0625 to 0.0625
- key_weight: bfloat16 [8192, 1024], P('batch'), may hold values from -0.0625 to 0.0625
- value_weight: bfloat16 [8192, 1024], P('batch'), may hold values from -0.0625 to 0.0625
Outputs:
- attended: bfloat16 [16384, 8192], P('batch', 'weight')
Inputs may be any that keep to these rules, and one draw needn't show every extreme that they name: `segment_ids`: segment ids never fall along the tokens; each id covers 1 to 64 consecutive tokens, one of them exactly 64.
All inputs are finite; a program needn't handle non-finite values.
Results may differ from a plain program's by a relative error of at most 0.0079.
Values may be sent and summed in bfloat16 or wider, within the bound.
No kernel may reach another device: no remote copies, remote signals or barrier semaphores. Data moves between devices by JAX's collectives and lax.ppermute only.
A program may use at most 64 MiB of HBM per device.

v0:
```python
import math
import jax
import jax.numpy as jnp
from jax import lax
from jax.sharding import PartitionSpec as P

HEADS = 64
KV_HEADS = 8
HEAD_DIM = 128
ROPE_BASE = 500000.0
EPSILON = 1e-05


def positions_in_segment(seg_ids):
    places = jnp.arange(seg_ids.shape[0], dtype=jnp.int32)
    earlier = jnp.concatenate([seg_ids[:1] - 1, seg_ids[:-1]])
    starts = jnp.where(seg_ids != earlier, places, 0)
    leading = lax.cummax(starts, axis=0)
    return places - leading


def rotate(vectors, positions):
    half_dim = vectors.shape[-1] // 2
    ratios = jnp.arange(half_dim, dtype=jnp.float32) * (2.0 / vectors.shape[-1])
    frequency = jnp.exp(-math.log(ROPE_BASE) * ratios)
    angles = positions.astype(jnp.float32)[:, None] * frequency[None, :]
    cosine = jnp.cos(angles)[:, None, :]
    sine_part = jnp.sin(angles)[:, None, :]
    front_half = vectors[..., :half_dim]
    back_half = vectors[..., half_dim:]
    return jnp.concatenate(
        [front_half * cosine - back_half * sine_part, back_half * cosine + front_half * sine_part],
        axis=-1,
    )


def attend(grouped, rotated_keys, value_rows, seg_ids):
    scores = jnp.einsum(
        "ingd,jnd->ngij", grouped, rotated_keys, preferred_element_type=jnp.float32
    ) * grouped.shape[-1] ** (-0.5)
    places = jnp.arange(seg_ids.shape[0], dtype=jnp.int32)
    allowed = (seg_ids[:, None] == seg_ids[None, :]) & (places[None, :] <= places[:, None])
    weights = jnp.where(allowed, jnp.exp(scores), 0.0)
    probabilities = (weights / jnp.sum(weights, axis=-1, keepdims=True)).astype(jnp.bfloat16)
    mixed = jnp.einsum(
        "ngij,jnd->ingd", probabilities, value_rows, preferred_element_type=jnp.float32
    )
    return mixed.astype(jnp.bfloat16)


def per_device(tokens, segment_ids, norm_gain, query_weight, key_weight, value_weight):
    head_dim = HEAD_DIM
    query_cols = query_weight.shape[1]
    heads_dev = query_cols // head_dim
    group_size = HEADS // KV_HEADS
    local_kv = max(1, heads_dev // group_size)
    first_kv = lax.axis_index("weight") * heads_dev // group_size
    key_width = local_kv * head_dim
    key_block = lax.dynamic_slice_in_dim(key_weight, first_kv * head_dim, key_width, 1)
    value_block = lax.dynamic_slice_in_dim(value_weight, first_kv * head_dim, key_width, 1)
    values = tokens.astype(jnp.float32)
    inverse_rms = lax.rsqrt(jnp.mean(values * values, axis=1, keepdims=True) + EPSILON)
    normed = (values * inverse_rms * norm_gain[None, :]).astype(jnp.bfloat16)
    local_weights = jnp.concatenate([query_weight, key_block, value_block], axis=1)
    full_weights = lax.all_gather(local_weights, "batch", axis=0, tiled=True)
    projected = jnp.dot(
        lax.all_gather(normed, "weight", axis=0, tiled=True),
        full_weights,
        preferred_element_type=jnp.float32,
    )
    query_part = projected[:, :query_cols]
    key_rows = projected[:, query_cols : query_cols + key_width].astype(jnp.bfloat16)
    value_rows = projected[:, query_cols + key_width :].astype(jnp.bfloat16)
    pack_rows = projected.shape[0]
    positions = positions_in_segment(segment_ids)
    queries = rotate(query_part.reshape(pack_rows, heads_dev, head_dim), positions).astype(
        jnp.bfloat16
    )
    rotated_keys = rotate(
        key_rows.astype(jnp.float32).reshape(pack_rows, local_kv, head_dim), positions
    ).astype(jnp.bfloat16)
    grouped = queries.reshape(pack_rows, local_kv, heads_dev // local_kv, head_dim)
    attended = attend(
        grouped, rotated_keys, value_rows.reshape(pack_rows, local_kv, head_dim), segment_ids
    )
    return attended.reshape(pack_rows, query_cols)


def solution(mesh):
    placed = (
        P(("batch", "weight"), None),
        P("batch"),
        P(),
        P("batch", "weight"),
        P("batch", None),
        P("batch", None),
    )
    return jax.shard_map(
        per_device, mesh=mesh, in_specs=placed, out_specs=P("batch", "weight"), check_vma=False
    )
```

profile of v0, /device:TPU:1, one launch (start us, length us, event | category | flops | bytes accessed | tf_op | source)
XLA Modules:
  0.0 284.9 jit_solution(18422892970738844618)
XLA Ops:
  6.5 1.2 fusion.7
  7.8 2.0 fusion.9
  9.9 0.9 constant_dynamic-slice_fusion
  10.8 1.7 pad_maximum_fusion
  12.6 1.3 slice.39
  14.5 0.8 select_bitcast_fusion
  15.3 0.3 reduce-window.9
  15.7 0.1 slice.41
  15.8 0.1 slice_reduce_fusion
  15.9 0.1 fusion.28
  16.0 1.0 fusion.10
  16.9 1.0 multiply_cosine_fusion
  17.9 55.4 %all-gather.3.cloned.1.call-done = bf16[512,8192]{1,0:T(8,128)(2,1)} async-done(((bf16[32,8192]{1,0:T(8,128)(2,1)}), bf16[512,8192]{1,0:T(8,128)(2,1)}) %all-gather.3.cloned.1.call-update) | async-done | bytes 8388624 | tf_op jit(solution)/shard_map/all_gather | solution.py:67
  73.4 183.1 %all-gather.5.cloned.1.call-done = bf16[8192,768]{1,0:T(8,128)(2,1)} async-done(((bf16[256,768]{1,0:T(8,128)(2,1)}), bf16[8192,768]{1,0:T(8,128)(2,1)}) %all-gather.5.cloned.1.call-update) | async-done | bytes 12582928 | tf_op jit(solution)/shard_map/all_gather | solution.py:65
  256.4 13.4 %fusion.33 = (bf16[512,768]{1,0:T(8,128)(2,1)}, f32[512,768]{1,0:T(8,128)S(1)}) fusion(bf16[512,8192]{1,0:T(8,128)(2,1)} %all-gather.3.cloned.1.call-done, bf16[8192,768]{1,0:T(8,128)(2,1)} %all-gather.5.cloned.1.call-done), kind=kOutput, calls=%fused_computation.54 | convolution fusion | flops 6442844160 | bytes 23330816 | tf_op jit(solution)/shard_map/dot_general | solution.py:66
  269.9 0.1 slice.51
  270.0 0.4 reshape.192
  270.4 0.6 fusion.32
  271.0 0.9 fusion.23
  271.9 1.2 fusion.27
  273.1 0.3 subtract_convert_fusion
  273.4 1.5 fusion
  274.9 2.2 fusion.4
  277.1 1.0 copy.16
  (7 shorter events, 0.1 us)
Async XLA Ops:
  6.5 66.8 %all-gather.3.cloned.1.call-start = ((), (), s32[]{:S(2)}) async-start(), calls=%async_computation | async-start | bytes 8912896 | tf_op jit(solution)/shard_map/all_gather | solution.py:67
  9.9 246.6 %all-gather.5.cloned.1.call-start = ((), (), s32[]{:S(2)}) async-start(), calls=%async_computation.1 | async-start | bytes 12976128 | tf_op jit(solution)/shard_map/all_gather | solution.py:65
Sparse Core Ops, SparseCore 0:
  10.0 63.3 all-gather.2
  76.5 179.8 all-gather.4
where the time goes:
time: 285 us
  waiting for transfers between devices  239 us (84%)
  matrix products  17.1 us (6%)
  between operations  14.2 us (5%)
  other arithmetic  10.7 us (4%)
  local copies, waits for them, and re-layouts  4.42 us (2%)
    all_gather x1, waiting for transfers between devices, per_device(): full_weights = lax.all_gather(local_weights, 'batch', axis=0, tiled=True)  183 us
    all_gather x1, waiting for transfers between devices, per_device(): lax.all_gather(normed, 'weight', axis=0, tiled=True)  55.4 us
    dot_general x1, matrix products, per_device(): jnp.dot(lax.all_gather(normed, 'weight', axis=0, tiled=True), full_weight...  13.4 us
  transfers between devices with their start and end apart: 2, of which 2 were waited for; matrix products, arithmetic and copies ran while one was open for 3% of the time, Pallas kernels for 0%

commit v1 on v0

--- a/solution.py
+++ b/solution.py
@@ -62,7 +62,9 @@
     inverse_rms = lax.rsqrt(jnp.mean(values * values, axis=1, keepdims=True) + EPSILON)
     normed = (values * inverse_rms * norm_gain[None, :]).astype(jnp.bfloat16)
     local_weights = jnp.concatenate([query_weight, key_block, value_block], axis=1)
-    full_weights = lax.all_gather(local_weights, "batch", axis=0, tiled=True)
+    full_weights = jnp.concatenate(
+        lax.all_to_all(jnp.stack([local_weights] * lax.axis_size("batch")), "batch", 0, 0), axis=0
+    )
     projected = jnp.dot(
         lax.all_gather(normed, "weight", axis=0, tiled=True),
         full_weights,

time: 285 us -> 509 us (1.79)
  the two profiles are of different devices: /device:TPU:1 before, /device:TPU:360 now
where the time goes in v1:
time: 509 us
  waiting for transfers between devices  450 us (88%)
  matrix products  17.2 us (3%)
  between operations  14.1 us (3%)
  starting transfers between devices  11.5 us (2%)
  local copies, waits for them, and re-layouts  9.63 us (2%)
  other arithmetic  6.33 us (1%)
    all_to_all x1, waiting for transfers between devices, per_device(): lax.all_to_all(jnp.stack([local_weights] * lax.axis_size('batch')), 'batc...  266 us
    all_gather x1, waiting for transfers between devices, per_device(): lax.all_gather(normed, 'weight', axis=0, tiled=True)  184 us
    dot_general x1, matrix products, per_device(): jnp.dot(lax.all_gather(normed, 'weight', axis=0, tiled=True), full_weight...  13.5 us
    all_to_all x1, starting transfers between devices, per_device(): lax.all_to_all(jnp.stack([local_weights] * lax.axis_size('batch')), 'batc...  11.5 us
  transfers between devices with their start and end apart: 2, of which 2 were waited for; matrix products, arithmetic and copies ran while one was open for 1% of the time, Pallas kernels for 0%

profile of v1, /device:TPU:360, one launch (start us, length us, event | category | flops | bytes accessed | tf_op | source)
XLA Modules:
  0.0 508.7 jit_solution(6105842424092136823)
XLA Ops:
  6.5 0.9 constant_dynamic-slice_fusion
  7.4 1.0 pad_maximum_fusion
  8.4 5.9 %stack.2 = bf16[32,256,768]{2,1,0:T(8,128)(2,1)} broadcast(bf16[256,768]{1,0:T(8,128)(2,1)S(1)} %pad_maximum_fusion), dimensions={1,2} | broadcast | bytes 12976128 | tf_op jit(solution)/shard_map/stack | solution.py:66
  14.3 11.5 %all-to-all-start = ((bf16[32,256,768]{2,1,0:T(8,128)(2,1)}), bf16[32,256,768]{2,1,0:T(8,128)(2,1)}, u32[]{:S(2)}, u32[]{:S(2)}) async-start(bf16[32,256,768]{2,1,0:T(8,128)(2,1)} %stack.2), calls=%async_computation | async-start | bytes 25165824 | tf_op jit(solution)/shard_map/all_to_all | solution.py:66
  25.9 0.2 fusion.7
  26.1 1.0 fusion.9
  27.1 0.5 slice.39
  28.3 0.1 select_bitcast_fusion
  28.4 0.3 reduce-window.9
  28.8 0.1 slice_reduce_fusion
  29.0 0.2 fusion.10
  29.2 1.0 multiply_cosine_fusion
  30.2 184.1 %all-gather.2.cloned.1.call-done = bf16[512,8192]{1,0:T(8,128)(2,1)} async-done(((bf16[32,8192]{1,0:T(8,128)(2,1)}), bf16[512,8192]{1,0:T(8,128)(2,1)}) %all-gather.2.cloned.1.call-update) | async-done | bytes 8388624 | tf_op jit(solution)/shard_map/all_gather | solution.py:69
  214.3 265.9 %all-to-all-done = bf16[32,256,768]{2,1,0:T(8,128)(2,1)} async-done(((bf16[32,256,768]{2,1,0:T(8,128)(2,1)}), bf16[32,256,768]{2,1,0:T(8,128)(2,1)}, u32[]{:S(2)}, u32[]{:S(2)}) %all-to-all-start) | async-done | bytes 12582944 | tf_op jit(solution)/shard_map/all_to_all | solution.py:66
  480.1 13.5 %fusion.33 = (bf16[512,768]{1,0:T(8,128)(2,1)}, f32[512,768]{1,0:T(8,128)S(1)}) fusion(bf16[512,8192]{1,0:T(8,128)(2,1)} %all-gather.2.cloned.1.call-done, bf16[8192,768]{1,0:T(8,128)(2,1)} %bitcast), kind=kOutput, calls=%fused_computation.54 | convolution fusion | flops 6442844160 | bytes 23330816 | tf_op jit(solution)/shard_map/dot_general | solution.py:68
  493.6 0.1 slice.51
  493.8 0.4 reshape.198
  494.1 0.6 fusion.32
  494.7 0.9 fusion.23
  495.7 1.2 fusion.27
  496.9 0.3 subtract_convert_fusion
  497.2 1.5 fusion
  498.6 2.2 fusion.4
  500.9 1.0 copy.16
  (13 shorter events, 0.3 us)
Async XLA Ops:
  14.3 11.6 %copy-start = (bf16[32,8192]{1,0:T(8,128)(2,1)S(1)}, bf16[32,8192]{1,0:T(8,128)(2,1)}, u32[]{:S(2)}) copy-start(bf16[32,8192]{1,0:T(8,128)(2,1)} %param.6) | copy-start | bytes 1572868
  14.3 11.8 %copy-start.2 = (f32[8192]{0:T(1024)S(1)}, f32[8192]{0:T(1024)}, u32[]{:S(2)}) copy-start(f32[8192]{0:T(1024)} %param.8) | copy-start | bytes 98308
  14.3 12.8 %copy-start.1 = (s32[512]{0:T(512)S(1)}, s32[512]{0:T(512)}, u32[]{:S(2)}) copy-start(s32[512]{0:T(512)} %param.7) | copy-start | bytes 6148
  14.3 465.8 %all-to-all-start = ((bf16[32,256,768]{2,1,0:T(8,128)(2,1)}), bf16[32,256,768]{2,1,0:T(8,128)(2,1)}, u32[]{:S(2)}, u32[]{:S(2)}) async-start(bf16[32,256,768]{2,1,0:T(8,128)(2,1)} %stack.2), calls=%async_computation | async-start | bytes 25165824 | tf_op jit(solution)/shard_map/all_to_all | solution.py:66
  25.8 188.5 %all-gather.2.cloned.1.call-start = ((), (), s32[]{:S(2)}) async-start(), calls=%async_computation.1 | async-start | bytes 8912896 | tf_op jit(solution)/shard_map/all_gather | solution.py:69
Sparse Core Ops, SparseCore 0:
  28.8 185.4 all-gather.1
